TPU v7x, 256 devices: a whole 4x4x8 slice. The times are simulated.
256 devices in a mesh: space: 32 (over x, y, core), tm: 8 (over z).
Axes of the slice: x: 4, y: 4, z: 8, core: 2. Of those that a mesh axis runs over, the one named last changes fastest.
Arguments:
- velocity: bfloat16 [256, 2, 512, 1024], P('tm', None, 'space'), may hold values from -8.4 to 8.4
Outputs:
- vorticity: bfloat16 [256, 512, 1024], P('tm', 'space')
- modes: float32 [32, 512, 1024], P('tm', 'space')
All inputs are finite; a program needn't handle non-finite values.
Results may differ from a plain program's by a relative error of at most 0.003.
Values may be sent and summed in bfloat16 or wider, within the bound.
A program may use at most 64 MiB of HBM per device.

v0:
```python
import jax
import jax.numpy as jnp
from jax import lax
from jax.sharding import PartitionSpec as P

RANK = 32


def extended(block, sides, width):
    for axis, dim in sides:
        count = lax.axis_size(axis)
        forward = [(i, i + 1) for i in range(count - 1)]
        forward.append((count - 1, 0))
        backward = [(target, source) for source, target in forward]
        low = lax.ppermute(
            lax.slice_in_dim(block, block.shape[dim] - width, None, axis=dim), axis, forward
        )
        high = lax.ppermute(lax.slice_in_dim(block, 0, width, axis=dim), axis, backward)
        block = jnp.concatenate([low, block, high], axis=dim)
    return block


def partner_2(value, axis, apart):
    mask = 2**apart
    pairs = [(source, source ^ mask) for source in range(lax.axis_size(axis))]
    return lax.ppermute(value, axis, pairs)


def merge_nodes(stacked):
    high = lax.Precision.HIGHEST
    gram = lax.psum(jnp.einsum("naxz,nbxz->nab", stacked, stacked, precision=high), "space")
    coeffs = gram[:, :, :RANK] + gram[:, :, RANK:]
    diagonal = jnp.diagonal(gram, axis1=1, axis2=2)
    scales = jnp.sqrt(diagonal[:, :RANK] + diagonal[:, RANK:])
    eye = jnp.broadcast_to(jnp.eye(RANK, dtype=jnp.float32), (stacked.shape[0], RANK, RANK))
    mixed = jnp.einsum("nab,naxz->nbxz", coeffs, stacked, precision=high)
    inner = lax.psum(jnp.einsum("naxz,nbxz->nab", mixed, mixed, precision=high), "space")
    lower = jnp.linalg.cholesky(inner)
    lower_inv = lax.linalg.triangular_solve(lower, eye, left_side=True, lower=True)
    factor = jnp.swapaxes(lower_inv, 1, 2) * scales[:, None, :]
    return jnp.einsum("nab,naxz->nbxz", factor, mixed, precision=high)


def spanwise(field):
    ahead = jnp.roll(field, -1, 2)
    behind = jnp.roll(field, 1, 2)
    ahead_two = jnp.roll(field, -2, 2)
    behind_two = jnp.roll(field, 2, 2)
    return (8.0 * (ahead - behind) - (ahead_two - behind_two)) / 12.0


def local(velocity):
    rows = velocity.shape[2]
    padded = extended(velocity, (("space", 2),), 2).astype(jnp.float32)
    stream_u = padded[:, 0, 2 : rows + 2]
    span_v = padded[:, 1]
    dv_dx = (
        8.0 * (span_v[:, 3 : rows + 3] - span_v[:, 1 : rows + 1])
        - (span_v[:, 4:] - span_v[:, :rows])
    ) / 12.0
    vorticity = (dv_dx - spanwise(stream_u)).astype(jnp.bfloat16)
    blocks = lax.axis_size("tm")
    levels = blocks.bit_length() - 1
    my_block = lax.axis_index("tm")
    share = RANK // blocks
    fields = vorticity.astype(jnp.float32)
    for level in range(levels):
        if level == 0:
            partner = partner_2(vorticity, "tm", 0).astype(jnp.float32)
        else:
            partner = partner_2(fields, "tm", level)
        upper = my_block // 2**level % 2 == 1
        first = jnp.where(upper, partner, fields)
        second = jnp.where(upper, fields, partner)
        fields = merge_nodes(jnp.concatenate([first, second], axis=0)[None])[0]
    modes = lax.dynamic_slice_in_dim(fields, my_block * share, share, 0)
    return (vorticity, modes)


def solution(mesh):
    in_specs = (P("tm", None, "space", None),)
    out_specs = (P("tm", "space", None), P("tm", "space", None))
    return jax.shard_map(local, mesh=mesh, in_specs=in_specs, out_specs=out_specs, check_vma=False)
```

profile of v0, /device:TPU:0, one launch (start us, length us, event | category | flops | bytes accessed | tf_op | source)
XLA Modules:
  0.0 1045.1 jit_solution(1491497612664828559)
XLA Ops:
  3.4 3.0 collective-permute-start.1
  6.4 3.9 collective-permute-done.1
  10.3 5.2 collective-permute-done
  22.5 15.7 %collective-permute-done.2 = bf16[32,16,1024]{2,0,1:T(8,128)(2,1)S(1)} collective-permute-done((bf16[32,16,1024]{2,0,1:T(8,128)(2,1)S(1)}, bf16[32,16,1024]{2,0,1:T(8,128)(2,1)S(1)}, u32[]{:S(2)}, u32[]{:S(2)}) %collective-permute-start.2) | collective-permute-done | bytes 1048608 | tf_op jit(solution)/shard_map/ppermute | solution.py:26
  40.8 3.4 fusion.14
  44.2 129.4 %psum.42 = f32[1,64,64]{2,1,0:T(8,128)S(1)} all-reduce(f32[1,64,64]{2,1,0:T(8,128)S(1)} %fusion.14), channel_id=1, replica_groups=mesh['space'=32,'tm'=8] {'space'}, use_global_device_ids=true, to_apply=%region_0.1 | all-reduce | flops 4096 | bytes 32768 | tf_op jit(solution)/shard_map/psum | solution.py:31
  173.6 4.2 fusion.4
  179.6 123.8 %psum.43 = f32[1,32,32]{1,2,0:T(8,128)S(1)} all-reduce(f32[1,32,32]{1,2,0:T(8,128)S(1)} %convolution_bitcast_fusion.5), channel_id=1, replica_groups=mesh['space'=32,'tm'=8] {'space'}, use_global_device_ids=true, to_apply=%region_1.2 | all-reduce | flops 1024 | bytes 8192 | tf_op jit(solution)/shard_map/psum | solution.py:37
  303.5 2.9 custom-call.16
  311.3 3.3 fusion.62
  314.6 3.3 collective-permute-start.3
  317.8 85.8 %collective-permute-done.3 = f32[32,16,1024]{2,0,1:T(8,128)S(1)} collective-permute-done((f32[32,16,1024]{2,0,1:T(8,128)}, f32[32,16,1024]{2,0,1:T(8,128)S(1)}, u32[]{:S(2)}, u32[]{:S(2)}) %collective-permute-start.3) | collective-permute-done | bytes 2097184 | tf_op jit(solution)/shard_map/ppermute | solution.py:26
  407.8 3.4 fusion.15
  411.2 125.6 %psum.44 = f32[1,64,64]{2,1,0:T(8,128)S(1)} all-reduce(f32[1,64,64]{2,1,0:T(8,128)S(1)} %fusion.15), channel_id=1, replica_groups=mesh['space'=32,'tm'=8] {'space'}, use_global_device_ids=true, to_apply=%region_4.7 | all-reduce | flops 4096 | bytes 32768 | tf_op jit(solution)/shard_map/psum | solution.py:31
  536.8 4.2 fusion.2
  542.8 123.8 %psum.45 = f32[1,32,32]{1,2,0:T(8,128)S(1)} all-reduce(f32[1,32,32]{1,2,0:T(8,128)S(1)} %convolution_bitcast_fusion.3), channel_id=1, replica_groups=mesh['space'=32,'tm'=8] {'space'}, use_global_device_ids=true, to_apply=%region_5.8 | all-reduce | flops 1024 | bytes 8192 | tf_op jit(solution)/shard_map/psum | solution.py:37
  666.6 2.9 custom-call.18
  674.4 3.3 fusion.63
  677.7 6.8 collective-permute-start.4
  686.1 85.1 %collective-permute-done.4 = f32[32,16,1024]{2,0,1:T(8,128)S(1)} collective-permute-done((f32[32,16,1024]{2,0,1:T(8,128)}, f32[32,16,1024]{2,0,1:T(8,128)S(1)}, u32[]{:S(2)}, u32[]{:S(2)}) %collective-permute-start.4) | collective-permute-done | bytes 2097184 | tf_op jit(solution)/shard_map/ppermute | solution.py:26
  775.3 3.4 fusion.16
  778.7 125.6 %psum.46 = f32[1,64,64]{2,1,0:T(8,128)S(1)} all-reduce(f32[1,64,64]{2,1,0:T(8,128)S(1)} %fusion.16), channel_id=1, replica_groups=mesh['space'=32,'tm'=8] {'space'}, use_global_device_ids=true, to_apply=%region_6.9 | all-reduce | flops 4096 | bytes 32768 | tf_op jit(solution)/shard_map/psum | solution.py:31
  904.4 4.2 fusion
  910.3 123.8 %psum.47 = f32[1,32,32]{1,2,0:T(8,128)S(1)} all-reduce(f32[1,32,32]{1,2,0:T(8,128)S(1)} %convolution_bitcast_fusion.1), channel_id=1, replica_groups=mesh['space'=32,'tm'=8] {'space'}, use_global_device_ids=true, to_apply=%region_7.10 | all-reduce | flops 1024 | bytes 8192 | tf_op jit(solution)/shard_map/psum | solution.py:37
  (63 shorter events, 47.9 us)
Async XLA Ops:
  3.4 6.9 collective-permute-start.1
  6.4 9.1 collective-permute-start
  20.5 17.7 %collective-permute-start.2 = (bf16[32,16,1024]{2,0,1:T(8,128)(2,1)S(1)}, bf16[32,16,1024]{2,0,1:T(8,128)(2,1)S(1)}, u32[]{:S(2)}, u32[]{:S(2)}) collective-permute-start(bf16[32,16,1024]{2,0,1:T(8,128)(2,1)S(1)} %fusion.9), channel_id=1, source_target_pairs={{0,1},{1,0},{2,3},{3,2},{4,5},{5,4},{6,7},{7,6},{8,9},{9,8},{10,11... | collective-permute-start | bytes 3145736 | tf_op jit(solution)/shard_map/ppermute | solution.py:26
  38.8 1.3 copy-start
  38.8 2.0 copy-start.1
  314.6 89.1 %collective-permute-start.3 = (f32[32,16,1024]{2,0,1:T(8,128)}, f32[32,16,1024]{2,0,1:T(8,128)S(1)}, u32[]{:S(2)}, u32[]{:S(2)}) collective-permute-start(f32[32,16,1024]{2,0,1:T(8,128)} %fusion.62), channel_id=1, source_target_pairs={{0,2},{1,3},{2,0},{3,1},{4,6},{5,7},{6,4},{7,5},{8,10},{9,11},{10,... | collective-permute-start | bytes 6291464 | tf_op jit(solution)/shard_map/ppermute | solution.py:26
  405.8 1.3 copy-start.2
  405.8 2.0 copy-start.3
  677.7 93.5 %collective-permute-start.4 = (f32[32,16,1024]{2,0,1:T(8,128)}, f32[32,16,1024]{2,0,1:T(8,128)S(1)}, u32[]{:S(2)}, u32[]{:S(2)}) collective-permute-start(f32[32,16,1024]{2,0,1:T(8,128)} %fusion.63), channel_id=1, source_target_pairs={{0,4},{1,5},{2,6},{3,7},{4,0},{5,1},{6,2},{7,3},{8,12},{9,13},{10,... | collective-permute-start | bytes 6291464 | tf_op jit(solution)/shard_map/ppermute | solution.py:26
  773.3 1.3 copy-start.4
  773.3 2.0 copy-start.5
where the time goes:
time: 1050 us
  blocking collectives  752 us (72%)
  waiting for transfers between devices  196 us (19%)
  matrix products  37.2 us (4%)
  other arithmetic  28.1 us (3%)
  local copies, waits for them, and re-layouts  15.8 us (2%)
  starting transfers between devices  15.1 us (1%)
    psum x3, blocking collectives, merge_nodes(): lax.psum(jnp.einsum('naxz,nbxz->nab', stacked, stacked, precision=high),...  381 us
    psum x3, blocking collectives, merge_nodes(): lax.psum(jnp.einsum('naxz,nbxz->nab', mixed, mixed, precision=high), 'spa...  371 us
    ppermute x3, waiting for transfers between devices, partner_2(): return lax.ppermute(value, axis, pairs)  187 us
  transfers between devices with their start and end apart: 5, of which 5 were waited for; matrix products, arithmetic and copies ran while one was open for 0% of the time, Pallas kernels for 0%

commit v1 on v0

--- a/solution.py
+++ b/solution.py
@@ -28,7 +28,9 @@
 
 def merge_nodes(stacked):
     high = lax.Precision.HIGHEST
-    gram = lax.psum(jnp.einsum("naxz,nbxz->nab", stacked, stacked, precision=high), "space")
+    x = jnp.einsum("naxz,nbxz->nab", stacked, stacked, precision=high)
+    parts = lax.all_gather(x, "space", axis=0, tiled=False)
+    gram = parts.sum(axis=0)
     coeffs = gram[:, :, :RANK] + gram[:, :, RANK:]
     diagonal = jnp.diagonal(gram, axis1=1, axis2=2)
     scales = jnp.sqrt(diagonal[:, :RANK] + diagonal[:, RANK:])

time: 1050 us -> 744 us (0.71)
  blocking collectives: 752 us -> 449 us
    psum x3 -> x0, blocking collectives: 381 us -> none  [merge_nodes(): lax.psum(jnp.einsum('naxz,nbxz->nab', stacked, stacked, precision=high),...]
    all_gather x0 -> x3, blocking collectives: none -> 69.4 us  [merge_nodes(): parts = lax.all_gather(x, 'space', axis=0, tiled=False)]
where the time goes in v1:
time: 744 us; the launch traced here: 736 us
  blocking collectives  449 us (60%)
  waiting for transfers between devices  196 us (26%)
  matrix products  37.3 us (5%)
  other arithmetic  28.4 us (4%)
  starting transfers between devices  15.3 us (2%)
  local copies, waits for them, and re-layouts  9.89 us (1%)
    psum x3, blocking collectives, merge_nodes(): lax.psum(jnp.einsum('naxz,nbxz->nab', mixed, mixed, precision=high), 'spa...  379 us
    ppermute x3, waiting for transfers between devices, partner_2(): return lax.ppermute(value, axis, pairs)  186 us
    all_gather x3, blocking collectives, merge_nodes(): parts = lax.all_gather(x, 'space', axis=0, tiled=False)  69.4 us
  transfers between devices with their start and end apart: 5, of which 5 were waited for; matrix products, arithmetic and copies ran while one was open for 0% of the time, Pallas kernels for 0%

profile of v1, /device:TPU:0, one launch (start us, length us, event | category | flops | bytes accessed | tf_op | source)
XLA Modules:
  0.0 736.4 jit_solution(6802546023524892588)
XLA Ops:
  3.4 3.0 collective-permute-start.1
  6.4 3.9 collective-permute-done.1
  10.3 5.2 collective-permute-done
  22.5 15.7 %collective-permute-done.2 = bf16[32,16,1024]{2,0,1:T(8,128)(2,1)S(1)} collective-permute-done((bf16[32,16,1024]{2,0,1:T(8,128)(2,1)S(1)}, bf16[32,16,1024]{2,0,1:T(8,128)(2,1)S(1)}, u32[]{:S(2)}, u32[]{:S(2)}) %collective-permute-start.2) | collective-permute-done | bytes 1048608 | tf_op jit(solution)/shard_map/ppermute | solution.py:26
  38.9 3.4 fusion.14
  42.3 25.4 %all-gather = f32[2048,64]{1,0:T(8,128)S(1)} all-gather(f32[64,64]{1,0:T(8,128)S(1)} %fusion.14), channel_id=2, replica_groups=mesh['space'=32,'tm'=8] {'space'}, dimensions={0}, use_global_device_ids=true | all-gather | bytes 540672 | tf_op jit(solution)/shard_map/all_gather | solution.py:32
  67.8 4.2 fusion.4
  73.8 126.4 %psum.21 = f32[1,32,32]{1,2,0:T(8,128)S(1)} all-reduce(f32[1,32,32]{1,2,0:T(8,128)S(1)} %convolution_bitcast_fusion.5), channel_id=1, replica_groups=mesh['space'=32,'tm'=8] {'space'}, use_global_device_ids=true, to_apply=%region_1.2 | all-reduce | flops 1024 | bytes 8192 | tf_op jit(solution)/shard_map/psum | solution.py:39
  200.3 2.9 custom-call.16
  208.1 3.3 fusion.62
  211.4 3.4 collective-permute-start.3
  214.8 85.8 %collective-permute-done.3 = f32[32,16,1024]{2,0,1:T(8,128)S(1)} collective-permute-done((f32[32,16,1024]{2,0,1:T(8,128)}, f32[32,16,1024]{2,0,1:T(8,128)S(1)}, u32[]{:S(2)}, u32[]{:S(2)}) %collective-permute-start.3) | collective-permute-done | bytes 2097184 | tf_op jit(solution)/shard_map/ppermute | solution.py:26
  302.7 3.4 fusion.15
  306.1 22.0 %all-gather.1 = f32[2048,64]{1,0:T(8,128)S(1)} all-gather(f32[64,64]{1,0:T(8,128)S(1)} %fusion.15), channel_id=3, replica_groups=mesh['space'=32,'tm'=8] {'space'}, dimensions={0}, use_global_device_ids=true | all-gather | bytes 540672 | tf_op jit(solution)/shard_map/all_gather | solution.py:32
  329.0 4.2 fusion.2
  335.0 126.4 %psum.22 = f32[1,32,32]{1,2,0:T(8,128)S(1)} all-reduce(f32[1,32,32]{1,2,0:T(8,128)S(1)} %convolution_bitcast_fusion.3), channel_id=1, replica_groups=mesh['space'=32,'tm'=8] {'space'}, use_global_device_ids=true, to_apply=%region_5.8 | all-reduce | flops 1024 | bytes 8192 | tf_op jit(solution)/shard_map/psum | solution.py:39
  461.5 2.9 custom-call.18
  468.5 3.3 fusion.63
  471.7 6.9 collective-permute-start.4
  480.2 84.9 %collective-permute-done.4 = f32[32,16,1024]{2,0,1:T(8,128)S(1)} collective-permute-done((f32[32,16,1024]{2,0,1:T(8,128)}, f32[32,16,1024]{2,0,1:T(8,128)S(1)}, u32[]{:S(2)}, u32[]{:S(2)}) %collective-permute-start.4) | collective-permute-done | bytes 2097184 | tf_op jit(solution)/shard_map/ppermute | solution.py:26
  567.3 3.4 fusion.16
  570.7 22.0 %all-gather.2 = f32[2048,64]{1,0:T(8,128)S(1)} all-gather(f32[64,64]{1,0:T(8,128)S(1)} %fusion.16), channel_id=4, replica_groups=mesh['space'=32,'tm'=8] {'space'}, dimensions={0}, use_global_device_ids=true | all-gather | bytes 540672 | tf_op jit(solution)/shard_map/all_gather | solution.py:32
  593.5 4.2 fusion
  599.6 126.6 %psum.23 = f32[1,32,32]{1,2,0:T(8,128)S(1)} all-reduce(f32[1,32,32]{1,2,0:T(8,128)S(1)} %convolution_bitcast_fusion.1), channel_id=1, replica_groups=mesh['space'=32,'tm'=8] {'space'}, use_global_device_ids=true, to_apply=%region_7.10 | all-reduce | flops 1024 | bytes 8192 | tf_op jit(solution)/shard_map/psum | solution.py:39
  (66 shorter events, 42.3 us)
Async XLA Ops:
  3.4 6.9 collective-permute-start.1
  6.4 9.1 %collective-permute-start = (bf16[32,2,2,1024]{3,0,2,1:T(8,128)(2,1)S(1)}, bf16[32,2,2,1024]{3,0,2,1:T(8,128)(2,1)S(1)}, u32[]{:S(2)}, u32[]{:S(2)}) collective-permute-start(bf16[32,2,2,1024]{3,0,2,1:T(8,128)(2,1)S(1)} %get-tuple-element.26), channel_id=1, source_target_pairs={{0,8},{8,16},{16,24},{24,32},{32,40},{40,48},{48,56},{56,64},{64,7... | collective-permute-start | bytes 786440 | tf_op jit(solution)/shard_map/ppermute | solution.py:15
  20.5 17.7 %collective-permute-start.2 = (bf16[32,16,1024]{2,0,1:T(8,128)(2,1)S(1)}, bf16[32,16,1024]{2,0,1:T(8,128)(2,1)S(1)}, u32[]{:S(2)}, u32[]{:S(2)}) collective-permute-start(bf16[32,16,1024]{2,0,1:T(8,128)(2,1)S(1)} %fusion.9), channel_id=1, source_target_pairs={{0,1},{1,0},{2,3},{3,2},{4,5},{5,4},{6,7},{7,6},{8,9},{9,8},{10,11... | collective-permute-start | bytes 3145736 | tf_op jit(solution)/shard_map/ppermute | solution.py:26
  38.8 3.4 copy-start
  38.8 3.4 copy-start.1
  211.4 89.2 %collective-permute-start.3 = (f32[32,16,1024]{2,0,1:T(8,128)}, f32[32,16,1024]{2,0,1:T(8,128)S(1)}, u32[]{:S(2)}, u32[]{:S(2)}) collective-permute-start(f32[32,16,1024]{2,0,1:T(8,128)} %fusion.62), channel_id=1, source_target_pairs={{0,2},{1,3},{2,0},{3,1},{4,6},{5,7},{6,4},{7,5},{8,10},{9,11},{10,... | collective-permute-start | bytes 6291464 | tf_op jit(solution)/shard_map/ppermute | solution.py:26
  302.7 3.4 copy-start.4
  302.7 3.4 copy-start.5
  471.7 93.4 %collective-permute-start.4 = (f32[32,16,1024]{2,0,1:T(8,128)}, f32[32,16,1024]{2,0,1:T(8,128)S(1)}, u32[]{:S(2)}, u32[]{:S(2)}) collective-permute-start(f32[32,16,1024]{2,0,1:T(8,128)} %fusion.63), channel_id=1, source_target_pairs={{0,4},{1,5},{2,6},{3,7},{4,0},{5,1},{6,2},{7,3},{8,12},{9,13},{10,... | collective-permute-start | bytes 6291464 | tf_op jit(solution)/shard_map/ppermute | solution.py:26
  567.3 3.4 copy-start.2
  567.3 3.4 copy-start.3
